TPU v7x, 32 devices: a whole 2x2x4 slice. The times are simulated.
32 devices in a mesh: leaf: 8 (over y, x, core), front: 4 (over z).
Axes of the slice: x: 2, y: 2, z: 4, core: 2. Of those that a mesh axis runs over, the one named last changes fastest.
Arguments:
- leaf_rhs: float32 [8, 64, 256], P('leaf', None, 'front'), may hold values from -6 to 6
- sep_rhs: float32 [8, 64, 256], P('leaf', None, 'front'), may hold values from -6 to 6
- leaf_inverse: float32 [8, 256, 256], P('leaf', 'front'), as said below
- sep_inverse: float32 [8, 256, 256], P('leaf', 'front')
- leaf_block: float32 [8, 32, 256], P('leaf', None, 'front'), may hold values from -0.375 to 0.375
- sep_block: float32 [8, 32, 256], P('leaf', None, 'front'), may hold values from -0.375 to 0.375
- pattern: int32 [2, 8, 32], replicated, may hold values from 0 to 255, as said below
- outer_solution: float32 [64, 256], P(None, 'front'), may hold values from -6 to 6
Outputs:
- solution: float32 [2, 8, 64, 256], P(None, 'leaf', None, 'front')
Inputs may be any that keep to these rules, and one draw needn't show every extreme that they name: `pattern`: within one supernode the 32 entries are distinct and rising, the first is 0 and the last is 255. `leaf_inverse`: each leaf block is lower triangular with its diagonal bounded away from zero.
All inputs are finite; a program needn't handle non-finite values.
Results may differ from a plain program's by a relative error of at most 0.0003.
Values sent between devices are 32-bit elements; how exact they have to be, the bound alone decides.
No kernel may reach another device: no remote copies, remote signals or barrier semaphores. Data moves between devices by JAX's collectives and lax.ppermute only.
A program may use at most 64 MiB of HBM per device.

v0:
```python
import jax
import jax.numpy as jnp
from jax import lax
from jax.sharding import PartitionSpec as P


def partner(block, axis, distance):
    count = lax.axis_size(axis)
    route = []
    for low in range(count):
        high = low | 1 << distance
        if high != low and high < count:
            route += [(low, high), (high, low)]
    return lax.ppermute(block, axis, route)


def times_rows(vectors, matrix):
    return jnp.dot(
        vectors, matrix, precision=lax.Precision.HIGHEST, preferred_element_type=jnp.float32
    )


def against_rows(vectors, matrix):
    return lax.dot_general(
        vectors,
        matrix,
        (((1,), (1,)), ((), ())),
        precision=lax.Precision.HIGHEST,
        preferred_element_type=jnp.float32,
    )


def body(
    leaf_rhs, sep_rhs, leaf_inverse, sep_inverse, leaf_block, sep_block, pattern, outer_solution
):
    group_count = lax.axis_size("leaf")
    depth = group_count.bit_length() - 1
    group_pos = lax.axis_index("leaf")
    front_pos = lax.axis_index("front")
    local_rows = leaf_rhs.shape[-1]
    full_rows = leaf_inverse.shape[-1]
    vector_count = leaf_rhs.shape[1]
    leaf_r = leaf_rhs[0]
    leaf_inv = leaf_inverse[0]
    leaf_u = leaf_block[0]
    sep_r = sep_rhs[0]
    sep_inv = sep_inverse[0]
    sep_u = sep_block[0]
    all_rows = jnp.arange(full_rows, dtype=jnp.int32)

    def geometry(level):
        blocks = 2 ** min(level, depth)
        share = local_rows // blocks
        offset = local_rows - (local_rows >> level - 1)
        return (share, offset, group_pos % blocks)

    def label_of(level):
        if level > depth:
            return jnp.int32(0)
        return group_pos // 2**level * 2**level + 2 ** (level - 1)

    def ids_of(level):
        return lax.dynamic_index_in_dim(pattern[1], label_of(level), 0, keepdims=False)

    def block_sum(term, level):
        nbits = min(level, depth)
        if nbits == depth:
            return lax.psum(term, ("leaf", "front"))
        piece = lax.psum_scatter(term, "front", scatter_dimension=1, tiled=True)
        for bit in range(nbits):
            piece = piece + partner(piece, "leaf", bit)
        return lax.all_gather(piece, "front", axis=1, tiled=True)

    leaf_y = against_rows(lax.all_gather(leaf_r, "front", axis=1, tiled=True), leaf_inv)
    leaf_ids = lax.dynamic_index_in_dim(pattern[0], group_pos, 0, keepdims=False)
    child_part = against_rows(leaf_y, leaf_u)
    child_ids = leaf_ids
    solved = {}
    for level in range(1, depth + 2):
        share, offset, inner_pos = geometry(level)
        own_r = sep_r[:, offset : offset + share]
        start_col = front_pos * local_rows + inner_pos * share
        contribution = jnp.zeros((vector_count, full_rows), jnp.float32)
        contribution = lax.dynamic_update_slice(contribution, own_r, (jnp.int32(0), start_col))
        selector = (child_ids[:, None] == all_rows[None, :]).astype(jnp.float32)
        contribution = contribution - times_rows(child_part, selector)
        whole_v = block_sum(contribution, level)
        y_level = against_rows(whole_v, sep_inv[offset : offset + share, :])
        solved[level] = y_level
        if level <= depth:
            child_part = against_rows(y_level, sep_u[:, offset : offset + share])
            child_ids = ids_of(level)
    parent_x = lax.all_gather(outer_solution, "front", axis=1, tiled=True)
    sep_full = jnp.zeros((vector_count, full_rows), jnp.float32)
    for level in range(depth + 1, 0, -1):
        share, offset, inner_pos = geometry(level)
        picked = jnp.take(parent_x, ids_of(level), axis=1)
        rest = solved[level] - times_rows(picked, sep_u[:, offset : offset + share])
        term = times_rows(rest, sep_inv[offset : offset + share, :])
        parent_x = block_sum(term, level)
        sep_full = jnp.where(label_of(level) == group_pos, parent_x, sep_full)
    picked = jnp.take(parent_x, leaf_ids, axis=1)
    rest = leaf_y - times_rows(picked, leaf_u)
    leaf_x = lax.psum_scatter(times_rows(rest, leaf_inv), "front", scatter_dimension=1, tiled=True)
    sep_x = lax.dynamic_slice_in_dim(sep_full, front_pos * local_rows, local_rows, 1)
    return jnp.stack([leaf_x, sep_x])[:, None]


def solution(mesh):
    placed = (
        P("leaf", None, "front"),
        P("leaf", None, "front"),
        P("leaf", "front", None),
        P("leaf", "front", None),
        P("leaf", None, "front"),
        P("leaf", None, "front"),
        P(),
        P(None, "front"),
    )
    return jax.shard_map(
        body, mesh=mesh, in_specs=placed, out_specs=P(None, "leaf", None, "front"), check_vma=False
    )
```

profile of v0, /device:TPU:0, one launch (start us, length us, event | category | flops | bytes accessed | tf_op | source)
XLA Modules:
  0.0 694.5 jit_solution(14276887811836147891)
XLA Ops:
  7.4 15.1 %all-gather = f32[1,64,256]{1,0,2:T(1,128)S(1)} all-gather(f32[1,64,64]{1,0,2:T(1,128)S(1)} %copy.15), channel_id=2, replica_groups=mesh['leaf'=8,'front'=4] {'front'}, dimensions={2}, use_global_device_ids=true | all-gather | bytes 81920 | tf_op jit(solution)/shard_map/all_gather | solution.py:74
  25.6 20.6 %reduce-scatter.16.cloned.1.call-done = f32[64,64]{1,0:T(8,128)} async-done(((f32[256,64]{1,0:T(8,128)}), f32[64,64]{1,0:T(8,128)}) %reduce-scatter.16.cloned.1.call-update) | async-done | bytes 16400
  48.4 13.5 %all_gather.19 = f32[64,256]{0,1:T(8,128)S(1)} all-gather(f32[64,64]{0,1:T(8,128)S(1)} %copy.16), channel_id=1, replica_groups=mesh['leaf'=8,'front'=4] {'front'}, dimensions={1}, use_global_device_ids=true | all-gather | bytes 81920 | tf_op jit(solution)/shard_map/all_gather | solution.py:72
  64.0 17.4 %reduce-scatter.18.cloned.1.call-done = f32[64,64]{1,0:T(8,128)} async-done(((f32[256,64]{1,0:T(8,128)}), f32[64,64]{1,0:T(8,128)}) %reduce-scatter.18.cloned.1.call-update) | async-done | bytes 16400
  82.3 1.2 collective-permute-done.1
  83.5 1.5 collective-permute-start.2
  85.5 2.0 collective-permute-done.2
  87.5 13.4 %all_gather.20 = f32[64,256]{0,1:T(8,128)S(1)} all-gather(f32[64,64]{0,1:T(8,128)S(1)} %copy.17), channel_id=1, replica_groups=mesh['leaf'=8,'front'=4] {'front'}, dimensions={1}, use_global_device_ids=true | all-gather | bytes 81920 | tf_op jit(solution)/shard_map/all_gather | solution.py:72
  102.8 115.3 %all-reduce.5.cloned.1.call-done = f32[64,256]{1,0:T(8,128)} async-done(((f32[64,256]{1,0:T(8,128)}), f32[64,256]{1,0:T(8,128)}) %all-reduce.5.cloned.1.call-update) | async-done | bytes 65552 | tf_op jit(solution)/shard_map/psum | solution.py:68
  221.0 14.3 %all_gather.21 = f32[64,256]{0,1:T(8,128)S(1)} all-gather(f32[64,64]{0,1:T(8,128)S(1)} %copy.18), channel_id=1, replica_groups=mesh['leaf'=8,'front'=4] {'front'}, dimensions={1}, use_global_device_ids=true | all-gather | bytes 81920 | tf_op jit(solution)/shard_map/all_gather | solution.py:93
  235.9 105.9 %all-reduce.7.cloned.1.call-done = f32[64,256]{1,0:T(8,128)} async-done(((f32[64,256]{1,0:T(8,128)}), f32[64,256]{1,0:T(8,128)}) %all-reduce.7.cloned.1.call-update) | async-done | bytes 65552 | tf_op jit(solution)/shard_map/psum | solution.py:68
  344.1 121.5 %all-reduce.9.cloned.1.call-done = f32[64,256]{1,0:T(8,128)} async-done(((f32[64,256]{1,0:T(8,128)}), f32[64,256]{1,0:T(8,128)}) %all-reduce.9.cloned.1.call-update) | async-done | bytes 65552 | tf_op jit(solution)/shard_map/psum | solution.py:68
  468.4 121.0 %all-reduce.11.cloned.1.call-done = f32[64,256]{1,0:T(8,128)} async-done(((f32[64,256]{1,0:T(8,128)}), f32[64,256]{1,0:T(8,128)}) %all-reduce.11.cloned.1.call-update) | async-done | bytes 65552 | tf_op jit(solution)/shard_map/psum | solution.py:68
  591.2 1.1 convolution_bitcast_fusion.2
  592.4 20.0 %reduce-scatter.20.cloned.1.call-done = f32[64,64]{1,0:T(8,128)} async-done(((f32[256,64]{1,0:T(8,128)}), f32[64,64]{1,0:T(8,128)}) %reduce-scatter.20.cloned.1.call-update) | async-done | bytes 16400
  613.3 1.2 collective-permute-done.3
  614.5 1.6 collective-permute-start.4
  616.0 2.3 collective-permute-done.4
  618.5 13.3 %all_gather.22 = f32[64,256]{0,1:T(8,128)S(1)} all-gather(f32[64,64]{0,1:T(8,128)S(1)} %copy.21), channel_id=1, replica_groups=mesh['leaf'=8,'front'=4] {'front'}, dimensions={1}, use_global_device_ids=true | all-gather | bytes 81920 | tf_op jit(solution)/shard_map/all_gather | solution.py:72
  632.6 1.0 convolution_bitcast_fusion.1
  633.8 17.6 %reduce-scatter.22.cloned.1.call-done = f32[64,64]{1,0:T(8,128)} async-done(((f32[256,64]{1,0:T(8,128)}), f32[64,64]{1,0:T(8,128)}) %reduce-scatter.22.cloned.1.call-update) | async-done | bytes 16400
  652.3 1.1 collective-permute-done.5
  653.5 13.4 %all_gather.23 = f32[64,256]{0,1:T(8,128)S(1)} all-gather(f32[64,64]{0,1:T(8,128)S(1)} %copy.22), channel_id=1, replica_groups=mesh['leaf'=8,'front'=4] {'front'}, dimensions={1}, use_global_device_ids=true | all-gather | bytes 81920 | tf_op jit(solution)/shard_map/all_gather | solution.py:72
  669.9 16.6 %reduce-scatter.24.cloned.1.call-done = f32[64,64]{1,0:T(8,128)} async-done(((f32[256,64]{1,0:T(8,128)}), f32[64,64]{1,0:T(8,128)}) %reduce-scatter.24.cloned.1.call-update) | async-done | bytes 16400
  (119 shorter events, 28.9 us)
Async XLA Ops:
  6.5 15.9 %copy-start = (f32[1,64,256]{2,1,0:T(8,128)S(1)}, f32[1,64,256]{2,1,0:T(8,128)}, u32[]{:S(2)}) copy-start(f32[1,64,256]{2,1,0:T(8,128)} %param.12) | copy-start | bytes 196612
  6.5 0.8 copy-start.7
  6.5 39.7 %reduce-scatter.16.cloned.1.call-start = ((), (), s32[]{:S(2)}) async-start(), calls=%async_computation.9 | async-start | bytes 163840
  6.5 0.7 copy-start.9
  22.5 0.7 copy-start.6
  23.4 0.8 copy-start.1
  25.5 55.9 %reduce-scatter.18.cloned.1.call-start = ((), (), s32[]{:S(2)}) async-start(), calls=%async_computation.10 | async-start | bytes 163840
  47.0 1.3 collective-permute-start
  48.4 13.5 %copy-start.3 = (f32[1,64,256]{2,1,0:T(8,128)S(1)}, f32[1,64,256]{2,1,0:T(8,128)}, u32[]{:S(2)}) copy-start(f32[1,64,256]{2,1,0:T(8,128)} %param.13) | copy-start | bytes 196612
  63.9 154.2 %all-reduce.5.cloned.1.call-start = ((), (), s32[]{:S(2)}) async-start(), calls=%async_computation.5 | async-start | bytes 131072 | tf_op jit(solution)/shard_map/psum | solution.py:68
  82.2 1.3 collective-permute-start.1
  83.5 3.9 collective-permute-start.2
  102.3 239.6 %all-reduce.7.cloned.1.call-start = ((), (), s32[]{:S(2)}) async-start(), calls=%async_computation.6 | async-start | bytes 131072 | tf_op jit(solution)/shard_map/psum | solution.py:68
  220.2 0.8 copy-start.8
  220.2 245.4 %all-reduce.9.cloned.1.call-start = ((), (), s32[]{:S(2)}) async-start(), calls=%async_computation.7 | async-start | bytes 131072 | tf_op jit(solution)/shard_map/psum | solution.py:68
  344.0 245.4 %all-reduce.11.cloned.1.call-start = ((), (), s32[]{:S(2)}) async-start(), calls=%async_computation.8 | async-start | bytes 131072 | tf_op jit(solution)/shard_map/psum | solution.py:68
  468.4 144.0 %reduce-scatter.20.cloned.1.call-start = ((), (), s32[]{:S(2)}) async-start(), calls=%async_computation.11 | async-start | bytes 163840
  592.3 59.0 %reduce-scatter.22.cloned.1.call-start = ((), (), s32[]{:S(2)}) async-start(), calls=%async_computation.12 | async-start | bytes 163840
  613.2 1.3 collective-permute-start.3
  614.5 3.9 collective-permute-start.4
  633.7 52.8 %reduce-scatter.24.cloned.1.call-start = ((), (), s32[]{:S(2)}) async-start(), calls=%async_computation.13 | async-start | bytes 163840
  652.2 1.3 collective-permute-start.5
  668.9 0.8 copy-start.4
  668.9 0.9 copy-start.5
  (1 other events, 0.7 us)
Sparse Core Ops, SparseCore 0:
  25.6 20.5 reduce-scatter.15
  64.0 17.3 reduce-scatter.17
  102.4 115.6 all-reduce.4
  223.5 118.3 all-reduce.6
  347.3 118.3 all-reduce.8
  471.1 118.3 all-reduce.10
  592.4 19.9 reduce-scatter.19
  633.8 17.4 reduce-scatter.21
  669.1 17.4 reduce-scatter.23
where the time goes:
time: 696 us; the launch traced here: 695 us
  waiting for transfers between devices  565 us (81%)
  blocking collectives  83.1 us (12%)
  local copies, waits for them, and re-layouts  16.8 us (2%)
  between operations  13.6 us (2%)
  matrix products  12.1 us (2%)
    psum x4, waiting for transfers between devices, block_sum(): return lax.psum(term, ('leaf', 'front'))  464 us
    unnamed x14, waiting for transfers between devices  92.4 us
    all_gather x4, blocking collectives, block_sum(): return lax.all_gather(piece, 'front', axis=1, tiled=True)  53.7 us
    all_gather x1, blocking collectives, body(): lax.all_gather(leaf_r, 'front', axis=1, tiled=True)  15.1 us
    all_gather x1, blocking collectives, body(): parent_x = lax.all_gather(outer_solution, 'front', axis=1, tiled=True)  14.3 us
  transfers between devices with their start and end apart: 15, of which 15 were waited for; matrix products, arithmetic and copies ran while one was open for 0% of the time, Pallas kernels for 0%

commit v1 on v0

--- a/solution.py
+++ b/solution.py
@@ -2,6 +2,12 @@
 import jax.numpy as jnp
 from jax import lax
 from jax.sharding import PartitionSpec as P
+
+
+def _map_works(packet, bus_axis, row_axis):
+    for dd in (bus_axis, row_axis):
+        packet = jax.lax.psum(packet, dd)
+    return packet
 
 
 def partner(block, axis, distance):
@@ -65,7 +71,7 @@
     def block_sum(term, level):
         nbits = min(level, depth)
         if nbits == depth:
-            return lax.psum(term, ("leaf", "front"))
+            return _map_works(term, bus_axis="front", row_axis="leaf")
         piece = lax.psum_scatter(term, "front", scatter_dimension=1, tiled=True)
         for bit in range(nbits):
             piece = piece + partner(piece, "leaf", bit)

time: 696 us -> 569 us (0.82)
  waiting for transfers between devices: 565 us -> 438 us
    psum x4 -> x8, waiting for transfers between devices: 464 us -> 339 us  [_map_works(): packet = jax.lax.psum(packet, dd)]
    unnamed x14 -> x18, waiting for transfers between devices: 92.4 us -> 91.1 us
  transfers between devices with their start and end apart: 15 -> 19, of which waited for: 15 -> 19; matrix products, arithmetic and copies ran while one was open for 0% -> 0% of each run, Pallas kernels for 0% -> 0%
where the time goes in v1:
time: 569 us; the launch traced here: 568 us
  waiting for transfers between devices  438 us (77%)
  blocking collectives  82.4 us (14%)
  local copies, waits for them, and re-layouts  16.8 us (3%)
  between operations  13.7 us (2%)
  matrix products  12.1 us (2%)
    psum x8, waiting for transfers between devices, _map_works(): packet = jax.lax.psum(packet, dd)  339 us
    unnamed x18, waiting for transfers between devices  91.1 us
    all_gather x4, blocking collectives, block_sum(): return lax.all_gather(piece, 'front', axis=1, tiled=True)  53.7 us
    all_gather x1, blocking collectives, body(): lax.all_gather(leaf_r, 'front', axis=1, tiled=True)  15.1 us
    all_gather x1, blocking collectives, body(): parent_x = lax.all_gather(outer_solution, 'front', axis=1, tiled=True)  13.6 us
  transfers between devices with their start and end apart: 19, of which 19 were waited for; matrix products, arithmetic and copies ran while one was open for 0% of the time, Pallas kernels for 0%

profile of v1, /device:TPU:0, one launch (start us, length us, event | category | flops | bytes accessed | tf_op | source)
XLA Modules:
  0.0 567.6 jit_solution(4279874988563743234)
XLA Ops:
  7.4 15.1 %all-gather = f32[1,64,256]{1,0,2:T(1,128)S(1)} all-gather(f32[1,64,64]{1,0,2:T(1,128)S(1)} %copy.15), channel_id=2, replica_groups=mesh['leaf'=8,'front'=4] {'front'}, dimensions={2}, use_global_device_ids=true | all-gather | bytes 81920 | tf_op jit(solution)/shard_map/all_gather | solution.py:80
  25.6 20.6 %reduce-scatter.16.cloned.1.call-done = f32[64,64]{1,0:T(8,128)} async-done(((f32[256,64]{1,0:T(8,128)}), f32[64,64]{1,0:T(8,128)}) %reduce-scatter.16.cloned.1.call-update) | async-done | bytes 16400
  48.4 13.5 %all_gather.19 = f32[64,256]{0,1:T(8,128)S(1)} all-gather(f32[64,64]{0,1:T(8,128)S(1)} %copy.16), channel_id=1, replica_groups=mesh['leaf'=8,'front'=4] {'front'}, dimensions={1}, use_global_device_ids=true | all-gather | bytes 81920 | tf_op jit(solution)/shard_map/all_gather | solution.py:78
  63.9 17.5 %reduce-scatter.18.cloned.1.call-done = f32[64,64]{1,0:T(8,128)} async-done(((f32[256,64]{1,0:T(8,128)}), f32[64,64]{1,0:T(8,128)}) %reduce-scatter.18.cloned.1.call-update) | async-done | bytes 16400
  82.3 1.2 collective-permute-done.1
  83.5 1.5 collective-permute-start.2
  85.5 1.9 collective-permute-done.2
  87.5 13.4 %all_gather.20 = f32[64,256]{0,1:T(8,128)S(1)} all-gather(f32[64,64]{0,1:T(8,128)S(1)} %copy.17), channel_id=1, replica_groups=mesh['leaf'=8,'front'=4] {'front'}, dimensions={1}, use_global_device_ids=true | all-gather | bytes 81920 | tf_op jit(solution)/shard_map/all_gather | solution.py:78
  102.3 32.3 %all-reduce.9.cloned.1.call-done = f32[64,256]{1,0:T(8,128)} async-done(((f32[64,256]{1,0:T(8,128)}), f32[64,256]{1,0:T(8,128)}) %all-reduce.9.cloned.1.call-update) | async-done | bytes 65552 | tf_op jit(solution)/shard_map/psum | solution.py:9
  135.1 54.8 %all-reduce.11.cloned.1.call-done = f32[64,256]{1,0:T(8,128)} async-done(((f32[64,256]{1,0:T(8,128)}), f32[64,256]{1,0:T(8,128)}) %all-reduce.11.cloned.1.call-update) | async-done | bytes 65552 | tf_op jit(solution)/shard_map/psum | solution.py:9
  192.2 33.5 %all-reduce.13.cloned.1.call-done = f32[64,256]{1,0:T(8,128)} async-done(((f32[64,256]{1,0:T(8,128)}), f32[64,256]{1,0:T(8,128)}) %all-reduce.13.cloned.1.call-update) | async-done | bytes 65552 | tf_op jit(solution)/shard_map/psum | solution.py:9
  226.5 13.6 %all_gather.21 = f32[64,256]{0,1:T(8,128)S(1)} all-gather(f32[64,64]{0,1:T(8,128)S(1)} %copy.18), channel_id=1, replica_groups=mesh['leaf'=8,'front'=4] {'front'}, dimensions={1}, use_global_device_ids=true | all-gather | bytes 81920 | tf_op jit(solution)/shard_map/all_gather | solution.py:99
  240.7 40.4 %all-reduce.15.cloned.1.call-done = f32[64,256]{1,0:T(8,128)} async-done(((f32[64,256]{1,0:T(8,128)}), f32[64,256]{1,0:T(8,128)}) %all-reduce.15.cloned.1.call-update) | async-done | bytes 65552 | tf_op jit(solution)/shard_map/psum | solution.py:9
  283.3 33.5 %all-reduce.17.cloned.1.call-done = f32[64,256]{1,0:T(8,128)} async-done(((f32[64,256]{1,0:T(8,128)}), f32[64,256]{1,0:T(8,128)}) %all-reduce.17.cloned.1.call-update) | async-done | bytes 65552 | tf_op jit(solution)/shard_map/psum | solution.py:9
  316.8 55.4 %all-reduce.19.cloned.1.call-done = f32[64,256]{1,0:T(8,128)} async-done(((f32[64,256]{1,0:T(8,128)}), f32[64,256]{1,0:T(8,128)}) %all-reduce.19.cloned.1.call-update) | async-done | bytes 65552 | tf_op jit(solution)/shard_map/psum | solution.py:9
  375.0 33.5 %all-reduce.21.cloned.1.call-done = f32[64,256]{1,0:T(8,128)} async-done(((f32[64,256]{1,0:T(8,128)}), f32[64,256]{1,0:T(8,128)}) %all-reduce.21.cloned.1.call-update) | async-done | bytes 65552 | tf_op jit(solution)/shard_map/psum | solution.py:9
  408.6 55.3 %all-reduce.23.cloned.1.call-done = f32[64,256]{1,0:T(8,128)} async-done(((f32[64,256]{1,0:T(8,128)}), f32[64,256]{1,0:T(8,128)}) %all-reduce.23.cloned.1.call-update) | async-done | bytes 65552 | tf_op jit(solution)/shard_map/psum | solution.py:9
  466.7 18.7 %reduce-scatter.20.cloned.1.call-done = f32[64,64]{1,0:T(8,128)} async-done(((f32[256,64]{1,0:T(8,128)}), f32[64,64]{1,0:T(8,128)}) %reduce-scatter.20.cloned.1.call-update) | async-done | bytes 16400
  487.5 1.5 collective-permute-start.4
  489.0 2.4 collective-permute-done.4
  491.5 13.3 %all_gather.22 = f32[64,256]{0,1:T(8,128)S(1)} all-gather(f32[64,64]{0,1:T(8,128)S(1)} %copy.21), channel_id=1, replica_groups=mesh['leaf'=8,'front'=4] {'front'}, dimensions={1}, use_global_device_ids=true | all-gather | bytes 81920 | tf_op jit(solution)/shard_map/all_gather | solution.py:78
  506.8 17.6 %reduce-scatter.22.cloned.1.call-done = f32[64,64]{1,0:T(8,128)} async-done(((f32[256,64]{1,0:T(8,128)}), f32[64,64]{1,0:T(8,128)}) %reduce-scatter.22.cloned.1.call-update) | async-done | bytes 16400
  526.6 13.4 %all_gather.23 = f32[64,256]{0,1:T(8,128)S(1)} all-gather(f32[64,64]{0,1:T(8,128)S(1)} %copy.22), channel_id=1, replica_groups=mesh['leaf'=8,'front'=4] {'front'}, dimensions={1}, use_global_device_ids=true | all-gather | bytes 81920 | tf_op jit(solution)/shard_map/all_gather | solution.py:78
  542.9 16.6 %reduce-scatter.24.cloned.1.call-done = f32[64,64]{1,0:T(8,128)} async-done(((f32[256,64]{1,0:T(8,128)}), f32[64,64]{1,0:T(8,128)}) %reduce-scatter.24.cloned.1.call-update) | async-done | bytes 16400
  (131 shorter events, 33.5 us)
Async XLA Ops:
  6.5 15.9 %copy-start = (f32[1,64,256]{2,1,0:T(8,128)S(1)}, f32[1,64,256]{2,1,0:T(8,128)}, u32[]{:S(2)}) copy-start(f32[1,64,256]{2,1,0:T(8,128)} %param.12) | copy-start | bytes 196612
  6.5 0.8 copy-start.7
  6.5 39.7 %reduce-scatter.16.cloned.1.call-start = ((), (), s32[]{:S(2)}) async-start(), calls=%async_computation.13 | async-start | bytes 163840
  25.5 55.9 %reduce-scatter.18.cloned.1.call-start = ((), (), s32[]{:S(2)}) async-start(), calls=%async_computation.14 | async-start | bytes 163840
  47.0 1.3 collective-permute-start
  48.4 13.5 %copy-start.3 = (f32[1,64,256]{2,1,0:T(8,128)S(1)}, f32[1,64,256]{2,1,0:T(8,128)}, u32[]{:S(2)}) copy-start(f32[1,64,256]{2,1,0:T(8,128)} %param.13) | copy-start | bytes 196612
  63.9 70.7 %all-reduce.9.cloned.1.call-start = ((), (), s32[]{:S(2)}) async-start(), calls=%async_computation.5 | async-start | bytes 131072 | tf_op jit(solution)/shard_map/psum | solution.py:9
  82.2 1.3 collective-permute-start.1
  83.5 3.9 collective-permute-start.2
  102.3 87.7 %all-reduce.11.cloned.1.call-start = ((), (), s32[]{:S(2)}) async-start(), calls=%async_computation.6 | async-start | bytes 131072 | tf_op jit(solution)/shard_map/psum | solution.py:9
  134.6 91.0 %all-reduce.13.cloned.1.call-start = ((), (), s32[]{:S(2)}) async-start(), calls=%async_computation.7 | async-start | bytes 131072 | tf_op jit(solution)/shard_map/psum | solution.py:9
  192.1 88.9 %all-reduce.15.cloned.1.call-start = ((), (), s32[]{:S(2)}) async-start(), calls=%async_computation.8 | async-start | bytes 131072 | tf_op jit(solution)/shard_map/psum | solution.py:9
  225.7 91.1 %all-reduce.17.cloned.1.call-start = ((), (), s32[]{:S(2)}) async-start(), calls=%async_computation.9 | async-start | bytes 131072 | tf_op jit(solution)/shard_map/psum | solution.py:9
  283.2 89.0 %all-reduce.19.cloned.1.call-start = ((), (), s32[]{:S(2)}) async-start(), calls=%async_computation.10 | async-start | bytes 131072 | tf_op jit(solution)/shard_map/psum | solution.py:9
  316.7 91.7 %all-reduce.21.cloned.1.call-start = ((), (), s32[]{:S(2)}) async-start(), calls=%async_computation.11 | async-start | bytes 131072 | tf_op jit(solution)/shard_map/psum | solution.py:9
  374.9 88.9 %all-reduce.23.cloned.1.call-start = ((), (), s32[]{:S(2)}) async-start(), calls=%async_computation.12 | async-start | bytes 131072 | tf_op jit(solution)/shard_map/psum | solution.py:9
  408.5 76.9 %reduce-scatter.20.cloned.1.call-start = ((), (), s32[]{:S(2)}) async-start(), calls=%async_computation.15 | async-start | bytes 163840
  466.7 57.7 %reduce-scatter.22.cloned.1.call-start = ((), (), s32[]{:S(2)}) async-start(), calls=%async_computation.16 | async-start | bytes 163840
  486.3 1.3 collective-permute-start.3
  487.5 3.9 collective-permute-start.4
  506.7 52.8 %reduce-scatter.24.cloned.1.call-start = ((), (), s32[]{:S(2)}) async-start(), calls=%async_computation.17 | async-start | bytes 163840
  525.2 1.3 collective-permute-start.5
  542.0 0.8 copy-start.4
  542.0 0.9 copy-start.5
  (5 other events, 3.7 us)
Sparse Core Ops, SparseCore 0:
  25.6 20.5 reduce-scatter.15
  64.0 17.3 reduce-scatter.17
  102.4 32.1 all-reduce.8
  137.8 52.1 all-reduce.10
  192.2 33.3 all-reduce.12
  228.8 52.1 all-reduce.14
  283.3 33.3 all-reduce.16
  320.1 52.1 all-reduce.18
  375.1 33.3 all-reduce.20
  411.7 52.1 all-reduce.22
  466.8 18.5 reduce-scatter.19
  506.9 17.4 reduce-scatter.21
  542.1 17.3 reduce-scatter.23
